TPU v7x, 256 devices: a whole 4x4x8 slice. The times are simulated.
256 devices in a mesh: fsdp: 32 (over x_hi, z, core), tp: 8 (over x_lo, y).
Axes of the slice: x: 4 (x_hi: 2, x_lo: 2; x = x_hi * 2 + x_lo), y: 4, z: 8, core: 2. Of those that a mesh axis runs over, the one named last changes fastest.
Arguments:
- hidden: bfloat16 [2048, 26624], P('fsdp', 'tp'), may hold values from -6 to 6
- out_grad: bfloat16 [2048, 16384], P('tp', 'fsdp'), may hold values from -6 to 6
- weight: bfloat16 [26624, 16384], P('tp', 'fsdp'), may hold values from -0.0390625 to 0.0390625
Outputs:
- hidden_grad: bfloat16 [2048, 26624], P('fsdp', 'tp')
- weight_grad: float32 [26624, 16384], P('tp', 'fsdp')
All inputs are finite; a program needn't handle non-finite values.
Results may differ from a plain program's by a relative error of at most 0.015.
Values may be sent and summed in bfloat16 or wider, within the bound.
No kernel may reach another device: no remote copies, remote signals or barrier semaphores. Data moves between devices by JAX's collectives and lax.ppermute only.
A program may use at most 128 MiB of HBM per device.

v0:
```python
import math
import jax
import jax.numpy as jnp
from jax import lax
from jax.sharding import PartitionSpec as P


def local(hidden, out_grad, weight):
    grad_rows = lax.all_gather(out_grad, "tp", axis=0, tiled=True)
    partial_sum = lax.dot_general(
        grad_rows, weight, (((1,), (1,)), ((), ())), preferred_element_type=jnp.float32
    )
    adjoint = lax.psum_scatter(
        partial_sum.astype(jnp.bfloat16), "fsdp", scatter_dimension=0, tiled=True
    ).astype(jnp.float32)
    hidden_grad = (adjoint + 0.5 * hidden.astype(jnp.float32)).astype(jnp.bfloat16)
    all_hidden = lax.all_gather(hidden, "fsdp", axis=0, tiled=True)
    weight_grad = lax.dot_general(
        all_hidden, grad_rows, (((0,), (0,)), ((), ())), preferred_element_type=jnp.float32
    )
    grad_scale = 1.0 / math.sqrt(grad_rows.shape[0])
    return (hidden_grad, weight_grad * grad_scale)


def solution(mesh):
    placed = (P("fsdp", "tp"), P("tp", "fsdp"), P("tp", "fsdp"))
    return jax.shard_map(
        local,
        mesh=mesh,
        in_specs=placed,
        out_specs=(P("fsdp", "tp"), P("tp", "fsdp")),
        check_vma=False,
    )
```

profile of v0, /device:TPU:1, one launch (start us, length us, event | category | flops | bytes accessed | tf_op | source)
XLA Modules:
  0.0 391.0 jit_solution(8042441853930988488)
XLA Ops:
  7.2 0.0 copy-start
  7.2 0.0 all-gather.3.cloned.1.call-start
  7.2 0.7 all-gather.3.cloned.1.call-update
  7.9 0.0 reduce-scatter.2.cloned.1.call-start
  8.0 44.1 %all-gather.3.cloned.1.call-done = bf16[2048,512]{1,0:T(8,128)(2,1)} async-done(((bf16[256,512]{1,0:T(8,128)(2,1)}), bf16[2048,512]{1,0:T(8,128)(2,1)}) %all-gather.3.cloned.1.call-update) | async-done | bytes 2097168 | tf_op jit(solution)/shard_map/all_gather | solution.py:9
  52.0 0.0 copy-done
  52.0 12.5 %convolution_convert_fusion = bf16[2048,3328]{1,0:T(8,128)(2,1)} fusion(bf16[2048,512]{1,0:T(8,128)(2,1)} %all-gather.3.cloned.1.call-done, bf16[3328,512]{1,0:T(8,128)(2,1)S(1)} %copy-done), kind=kOutput, calls=%fused_computation | convolution fusion | flops 6986137600 | bytes 19136512 | tf_op jit(solution)/shard_map/dot_general | solution.py:10
  64.5 0.0 reduce-scatter.2.cloned.1.call-update
  64.5 0.0 all-gather.5.cloned.1.call-start
  64.6 0.7 all-gather.5.cloned.1.call-update
  65.3 178.9 %reduce-scatter.2.cloned.1.call-done = bf16[64,3328]{1,0:T(8,128)(2,1)} async-done(((bf16[2048,3328]{1,0:T(8,128)(2,1)}), bf16[64,3328]{1,0:T(8,128)(2,1)}) %reduce-scatter.2.cloned.1.call-update) | async-done | bytes 426000 | tf_op jit(solution)/shard_map/reduce_scatter | solution.py:13
  244.2 2.0 add_convert_fusion
  246.2 125.5 %all-gather.5.cloned.1.call-done = bf16[2048,3328]{1,0:T(8,128)(2,1)} async-done(((bf16[64,3328]{1,0:T(8,128)(2,1)}), bf16[2048,3328]{1,0:T(8,128)(2,1)}) %all-gather.5.cloned.1.call-update) | async-done | bytes 13631504 | tf_op jit(solution)/shard_map/all_gather | solution.py:17
  371.7 12.8 %convolution_multiply_fusion = f32[3328,512]{1,0:T(8,128)} fusion(bf16[2048,3328]{1,0:T(8,128)(2,1)} %all-gather.5.cloned.1.call-done, bf16[2048,512]{1,0:T(8,128)(2,1)} %all-gather.3.cloned.1.call-done), kind=kOutput, calls=%fused_computation.1 | convolution fusion | flops 6981025792 | bytes 22544384 | tf_op jit(solution)/shard_map/dot_general | solution.py:18
Async XLA Ops:
  7.2 44.9 %copy-start = (bf16[3328,512]{1,0:T(8,128)(2,1)S(1)}, bf16[3328,512]{1,0:T(8,128)(2,1)}, u32[]{:S(2)}) copy-start(bf16[3328,512]{1,0:T(8,128)(2,1)} %param.5) | copy-start | bytes 10223620
  7.2 44.9 %all-gather.3.cloned.1.call-start = ((), (), s32[]{:S(2)}) async-start(), calls=%async_computation.1 | async-start | bytes 2359296 | tf_op jit(solution)/shard_map/all_gather | solution.py:9
  7.9 236.2 %reduce-scatter.2.cloned.1.call-start = ((), (), s32[]{:S(2)}) async-start(), calls=%async_computation.2 | async-start | bytes 14057472 | tf_op jit(solution)/shard_map/reduce_scatter | solution.py:13
  64.5 307.1 %all-gather.5.cloned.1.call-start = ((), (), s32[]{:S(2)}) async-start(), calls=%async_computation.3 | async-start | bytes 14057472 | tf_op jit(solution)/shard_map/all_gather | solution.py:17
Sparse Core Ops, SparseCore 0:
  9.8 42.2 all-gather.2
  64.7 179.4 reduce-scatter.1
  246.9 124.6 all-gather.4
where the time goes:
time: 391 us
  waiting for transfers between devices  350 us (90%)
  matrix products  25.2 us (6%)
  between operations  13.8 us (4%)
    reduce_scatter x1, waiting for transfers between devices, local(): lax.psum_scatter(partial_sum.astype(jnp.bfloat16), 'fsdp', scatter_dimens...  179 us
    all_gather x1, waiting for transfers between devices, local(): all_hidden = lax.all_gather(hidden, 'fsdp', axis=0, tiled=True)  125 us
    all_gather x1, waiting for transfers between devices, local(): grad_rows = lax.all_gather(out_grad, 'tp', axis=0, tiled=True)  44.1 us
    dot_general x1, matrix products, local(): lax.dot_general(all_hidden, grad_rows, (((0,), (0,)), ((), ())), preferre...  12.8 us
    dot_general x1, matrix products, local(): lax.dot_general(grad_rows, weight, (((1,), (1,)), ((), ())), preferred_el...  12.5 us
  transfers between devices with their start and end apart: 3, of which 3 were waited for; matrix products, arithmetic and copies ran while one was open for 1% of the time, Pallas kernels for 0%

commit v1 on v0

--- a/solution.py
+++ b/solution.py
@@ -6,7 +6,13 @@
 
 
 def local(hidden, out_grad, weight):
-    grad_rows = lax.all_gather(out_grad, "tp", axis=0, tiled=True)
+
+    def _push_chains(patch):
+        built = jnp.stack(jax.lax.psum(1, "tp") * [patch])
+        m_next = jax.lax.all_to_all(built, "tp", 0, 0)
+        return jnp.concatenate(m_next, axis=0)
+
+    grad_rows = _push_chains(out_grad)
     partial_sum = lax.dot_general(
         grad_rows, weight, (((1,), (1,)), ((), ())), preferred_element_type=jnp.float32
     )

time: 391 us -> 376 us (0.962)
  waiting for transfers between devices: 350 us -> 302 us
  blocking collectives: 0 us -> 31.5 us
    all_gather x1 -> x0, waiting for transfers between devices: 44.1 us -> none  [local(): grad_rows = lax.all_gather(out_grad, 'tp', axis=0, tiled=True)]
    all_to_all x0 -> x1, blocking collectives: none -> 31.5 us  [_push_chains(): m_next = jax.lax.all_to_all(built, 'tp', 0, 0)]
  transfers between devices with their start and end apart: 3 -> 2, of which waited for: 3 -> 2; matrix products, arithmetic and copies ran while one was open for 1% -> 1% of each run, Pallas kernels for 0% -> 0%
where the time goes in v1:
time: 376 us
  waiting for transfers between devices  302 us (80%)
  blocking collectives  31.5 us (8%)
  matrix products  23.2 us (6%)
  between operations  14.1 us (4%)
    reduce_scatter x1, waiting for transfers between devices, local(): lax.psum_scatter(partial_sum.astype(jnp.bfloat16), 'fsdp', scatter_dimens...  176 us
    all_gather x1, waiting for transfers between devices, local(): all_hidden = lax.all_gather(hidden, 'fsdp', axis=0, tiled=True)  125 us
    all_to_all x1, blocking collectives, _push_chains(): m_next = jax.lax.all_to_all(built, 'tp', 0, 0)  31.5 us
    dot_general x1, matrix products, local(): lax.dot_general(all_hidden, grad_rows, (((0,), (0,)), ((), ())), preferre...  12.8 us
    dot_general x1, matrix products, local(): lax.dot_general(grad_rows, weight, (((1,), (1,)), ((), ())), preferred_el...  10.4 us
  transfers between devices with their start and end apart: 2, of which 2 were waited for; matrix products, arithmetic and copies ran while one was open for 1% of the time, Pallas kernels for 0%

profile of v1, /device:TPU:1, one launch (start us, length us, event | category | flops | bytes accessed | tf_op | source)
XLA Modules:
  0.0 375.8 jit_solution(5507746861522302673)
XLA Ops:
  7.2 0.0 copy-start
  7.2 0.0 reduce-scatter.2.cloned.1.call-start
  7.2 1.3 stack.2
  8.5 31.5 %all_to_all.5 = bf16[8,256,512]{2,1,0:T(8,128)(2,1)S(1)} all-to-all(bf16[8,256,512]{2,1,0:T(8,128)(2,1)S(1)} %stack.2), channel_id=1, replica_groups=mesh['fsdp'=32,'tp'=8] {'tp'}, dimensions={0} | all-to-all | bytes 4194304 | tf_op jit(solution)/shard_map/all_to_all | solution.py:12
  40.0 0.0 copy-start.1
  40.0 1.3 copy-done.1
  41.3 0.0 copy-done
  41.3 10.4 %convolution_convert_fusion = bf16[2048,3328]{1,0:T(8,128)(2,1)} fusion(bf16[2048,512]{1,0:T(8,128)(2,1)S(1)} %bitcast.5, bf16[3328,512]{1,0:T(8,128)(2,1)S(1)} %copy-done), kind=kOutput, calls=%fused_computation | convolution fusion | flops 6986137600 | bytes 19136512 | tf_op jit(solution)/shard_map/dot_general | solution.py:16
  51.7 0.0 reduce-scatter.2.cloned.1.call-update
  51.7 0.0 all-gather.2.cloned.1.call-start
  51.7 0.7 all-gather.2.cloned.1.call-update
  52.4 176.3 %reduce-scatter.2.cloned.1.call-done = bf16[64,3328]{1,0:T(8,128)(2,1)} async-done(((bf16[2048,3328]{1,0:T(8,128)(2,1)}), bf16[64,3328]{1,0:T(8,128)(2,1)}) %reduce-scatter.2.cloned.1.call-update) | async-done | bytes 426000 | tf_op jit(solution)/shard_map/reduce_scatter | solution.py:19
  228.7 2.0 add_convert_fusion
  230.8 125.3 %all-gather.2.cloned.1.call-done = bf16[2048,3328]{1,0:T(8,128)(2,1)} async-done(((bf16[64,3328]{1,0:T(8,128)(2,1)}), bf16[2048,3328]{1,0:T(8,128)(2,1)}) %all-gather.2.cloned.1.call-update) | async-done | bytes 13631504 | tf_op jit(solution)/shard_map/all_gather | solution.py:23
  356.1 12.8 %convolution_multiply_fusion = f32[3328,512]{1,0:T(8,128)} fusion(bf16[2048,3328]{1,0:T(8,128)(2,1)} %all-gather.2.cloned.1.call-done, bf16[2048,512]{1,0:T(8,128)(2,1)} %bitcast.6), kind=kOutput, calls=%fused_computation.1 | convolution fusion | flops 6981025792 | bytes 22544384 | tf_op jit(solution)/shard_map/dot_general | solution.py:24
Async XLA Ops:
  7.2 34.1 %copy-start = (bf16[3328,512]{1,0:T(8,128)(2,1)S(1)}, bf16[3328,512]{1,0:T(8,128)(2,1)}, u32[]{:S(2)}) copy-start(bf16[3328,512]{1,0:T(8,128)(2,1)} %param.5) | copy-start | bytes 10223620
  7.2 221.6 %reduce-scatter.2.cloned.1.call-start = ((), (), s32[]{:S(2)}) async-start(), calls=%async_computation.2 | async-start | bytes 14057472 | tf_op jit(solution)/shard_map/reduce_scatter | solution.py:19
  40.0 1.3 copy-start.1
  51.7 304.4 %all-gather.2.cloned.1.call-start = ((), (), s32[]{:S(2)}) async-start(), calls=%async_computation.3 | async-start | bytes 14057472 | tf_op jit(solution)/shard_map/all_gather | solution.py:23
Sparse Core Ops, SparseCore 0:
  51.8 176.8 reduce-scatter.1
  231.5 124.5 all-gather.1
